TPU v7x, 32 devices: a whole 2x2x4 slice. The times are simulated.
32 devices in a mesh: groups: 2 (over y), frame: 4 (over z), quarter: 2 (over x), sub: 2 (over core).
Axes of the slice: x: 2, y: 2, z: 4, core: 2. Of those that a mesh axis runs over, the one named last changes fastest.
Arguments:
- queries: bfloat16 [16, 1024, 256], P(('groups', 'frame'), ('quarter', 'sub')), parts along dimension 0, may hold values from -36 to 36
- keys: bfloat16 [16, 1024, 256], P(('groups', 'frame'), ('quarter', 'sub')), parts along dimension 0, may hold values from -6 to 6
- values: bfloat16 [16, 1024, 256], P(('groups', 'frame'), ('quarter', 'sub')), parts along dimension 0, may hold values from -6 to 6
Outputs:
- attended: bfloat16 [16, 1024, 256], P(('groups', 'frame'), ('quarter', 'sub')), parts along dimension 0
There are 2 independent parts, one for each index of `groups`. A program takes and returns all parts, laid end to end along the dimension named above; each array names one. Nothing has to cross between parts.
All inputs are finite; a program needn't handle non-finite values.
Results may differ from a plain program's by a relative error of at most 0.0028.
Values may be sent and summed in bfloat16 or wider, within the bound.
A program may use at most 64 MiB of HBM per device.

v0:
```python
import math
import jax
import jax.numpy as jnp
from jax import lax
from jax.sharding import PartitionSpec as P

STRIP = 16


def partial_attend(query_rows, key_rows, value_rows, running, score_scale):
    top_run, sum_run, acc_run = running
    scores = (
        jnp.einsum("frd,fnd->frn", query_rows, key_rows, preferred_element_type=jnp.float32)
        * score_scale
    )
    highest = jnp.maximum(top_run, jnp.max(scores, axis=-1, keepdims=True))
    expo = jnp.exp(scores - highest)
    factor = jnp.exp(top_run - highest)
    sum_next = sum_run * factor + jnp.sum(expo, axis=-1, keepdims=True)
    acc_next = acc_run * factor + jnp.einsum(
        "frn,fnd->frd", expo.astype(jnp.bfloat16), value_rows, preferred_element_type=jnp.float32
    )
    return (highest, sum_next, acc_next)


def fold_keys(query_rows, score_scale, running, pieces):
    key_piece, value_piece = pieces
    length = key_piece.shape[1]
    block_keys = math.gcd(length, 2048)
    for block_index in range(length // block_keys):
        lower = block_index * block_keys
        running = partial_attend(
            query_rows,
            key_piece[:, lower : lower + block_keys],
            value_piece[:, lower : lower + block_keys],
            running,
            score_scale,
        )
    return running


def empty_state(query_rows):
    frames_here, rows_here, width = query_rows.shape
    return (
        jnp.full((frames_here, rows_here, 1), -jnp.inf, jnp.float32),
        jnp.zeros((frames_here, rows_here, 1), jnp.float32),
        jnp.zeros((frames_here, rows_here, width), jnp.float32),
    )


def body(queries, keys, values):
    head_width = queries.shape[2] // 2
    frames_dev = queries.shape[0]
    tokens_dev = queries.shape[1]
    score_scale = 1.0 / math.sqrt(head_width)
    query_spatial = queries[:, :, :head_width]
    key_spatial = keys[:, :, :head_width]
    value_spatial = values[:, :, :head_width]
    frame_count = lax.axis_size("frame")
    local_strips = tokens_dev // (STRIP * frame_count)

    def to_strips(array):
        part_two = array[:, :, head_width:].reshape(
            frames_dev, frame_count, local_strips, STRIP, head_width
        )
        return part_two.transpose(1, 2, 0, 3, 4)

    query_strip = lax.all_to_all(
        to_strips(queries), "frame", split_axis=0, concat_axis=2, tiled=True
    )
    key_strip = lax.all_to_all(to_strips(keys), "frame", split_axis=0, concat_axis=2, tiled=True)
    value_strip = lax.all_to_all(
        to_strips(values), "frame", split_axis=0, concat_axis=2, tiled=True
    )
    item_count = query_strip.shape[1]
    frames_all = query_strip.shape[2]
    rows_strip = frames_all * STRIP
    query_flat = query_strip.reshape(item_count, rows_strip, head_width)
    key_flat = key_strip.reshape(item_count, rows_strip, head_width)
    value_flat = value_strip.reshape(item_count, rows_strip, head_width)
    scores = (
        jnp.einsum("nqd,nkd->nqk", query_flat, key_flat, preferred_element_type=jnp.float32)
        * score_scale
    )
    highest = jnp.max(scores, axis=-1, keepdims=True)
    expo = jnp.exp(scores - highest)
    totals = jnp.sum(expo, axis=-1, keepdims=True)
    mixed = jnp.einsum(
        "nqk,nkd->nqd", expo.astype(jnp.bfloat16), value_flat, preferred_element_type=jnp.float32
    )
    strip_out = (
        (mixed / totals).astype(jnp.bfloat16).reshape(1, item_count, frames_all, STRIP, head_width)
    )
    returned = lax.all_to_all(strip_out, "frame", split_axis=2, concat_axis=0, tiled=True)
    temporal = returned.transpose(2, 0, 1, 3, 4).reshape(frames_dev, tokens_dev, head_width)
    top_all, total_spatial, acc_spatial = fold_keys(
        query_spatial,
        score_scale,
        empty_state(query_spatial),
        (
            lax.all_gather(key_spatial, ("quarter", "sub"), axis=1, tiled=True),
            lax.all_gather(value_spatial, ("quarter", "sub"), axis=1, tiled=True),
        ),
    )
    spatial = (acc_spatial / total_spatial).astype(jnp.bfloat16)
    return jnp.concatenate([spatial, temporal], axis=-1)


def solution(mesh):
    in_specs = (
        P(("groups", "frame"), ("quarter", "sub"), None),
        P(("groups", "frame"), ("quarter", "sub"), None),
        P(("groups", "frame"), ("quarter", "sub"), None),
    )
    out_specs = P(("groups", "frame"), ("quarter", "sub"), None)
    return jax.shard_map(body, mesh=mesh, in_specs=in_specs, out_specs=out_specs, check_vma=False)
```

profile of v0, /device:TPU:0, one launch (start us, length us, event | category | flops | bytes accessed | tf_op | source)
XLA Modules:
  0.0 53.8 jit_solution(1499810248122373728)
XLA Ops:
  0.0 1.0 %fusion.16 = (bf16[2,256,128]{2,1,0:T(8,128)(2,1)S(1)}, bf16[2,256,128]{2,1,0:T(8,128)(2,1)S(1)}) fusion(bf16[2,256,256]{2,1,0:T(8,128)(2,1)} %param.4), kind=kLoop, calls=%fused_computation.22 | loop fusion | bytes 524288 | tf_op jit(solution)/shard_map/slice | solution.py:57
  1.0 0.0 copy-start
  1.0 0.7 %copy.31 = bf16[4,4,2,16,128]{4,3,2,1,0:T(8,128)(2,1)} copy(bf16[4,4,2,16,128]{4,3,1,0,2:T(8,128)(2,1)S(1)} %bitcast.42) | data formatting | bytes 262144 | tf_op jit(solution)/shard_map/transpose | solution.py:66
  1.7 6.3 %all-to-all-start.1 = ((bf16[4,4,2,16,128]{4,3,2,1,0:T(8,128)(2,1)}), bf16[4,4,2,16,128]{4,3,2,1,0:T(8,128)(2,1)S(1)}, u32[]{:S(2)}, u32[]{:S(2)}) async-start(bf16[4,4,2,16,128]{4,3,2,1,0:T(8,128)(2,1)} %copy.31), calls=%async_computation.1 | async-start | bytes 262144 | tf_op jit(solution)/shard_map/all_to_all | solution.py:71
  8.0 0.0 slice-start
  8.0 7.3 %all_gather.6 = bf16[2,1024,128]{2,1,0:T(8,128)(2,1)S(1)} all-gather(bf16[2,256,128]{2,1,0:T(8,128)(2,1)S(1)} %get-tuple-element.5), channel_id=1, replica_groups=mesh['groups'=2,'frame'=4,'quarter'=2,'sub'=2] {'quarter','sub'}, dimensions={1}, use_global_device_ids=true | all-gather | bytes 655360 | tf_op jit(solution)/shard_map/all_gather | solution.py:101
  15.3 1.4 %multiply_reduce_fusion = (f32[2,256]{1,0:T(2,128)S(1)}, f32[2,256,1024]{2,1,0:T(8,128)S(1)}) fusion(bf16[2,1024,128]{2,1,0:T(8,128)(2,1)S(1)} %all_gather.6, bf16[2,256,256]{2,1,0:T(8,128)(2,1)} %param.3), kind=kOutput, calls=%fused_computation.1 | convolution fusion | flops 135265792 | bytes 2754560 | tf_op jit(solution)/shard_map/frd,fnd->frn/dot_general | solution.py:13
  16.7 0.0 copy-done
  16.8 0.1 copy.43
  16.9 0.0 slice-done
  16.9 0.7 %copy.29 = bf16[4,4,2,16,128]{4,3,2,1,0:T(8,128)(2,1)} copy(bf16[4,4,2,16,128]{4,3,1,0,2:T(8,128)(2,1)S(1)} %bitcast.37) | data formatting | bytes 262144 | tf_op jit(solution)/shard_map/transpose | solution.py:66
  17.6 0.7 %copy.33 = bf16[4,4,2,16,128]{4,3,2,1,0:T(8,128)(2,1)} copy(bf16[4,4,2,16,128]{4,3,1,0,2:T(8,128)(2,1)S(1)} %bitcast.41) | data formatting | bytes 262144 | tf_op jit(solution)/shard_map/transpose | solution.py:66
  18.2 0.5 fusion
  18.7 0.0 all-to-all-done.1
  18.7 5.1 %all-to-all-start = ((bf16[4,4,2,16,128]{4,3,2,1,0:T(8,128)(2,1)}), bf16[4,4,2,16,128]{4,3,2,1,0:T(8,128)(2,1)S(1)}, u32[]{:S(2)}, u32[]{:S(2)}) async-start(bf16[4,4,2,16,128]{4,3,2,1,0:T(8,128)(2,1)} %copy.29), calls=%async_computation | async-start | bytes 262144 | tf_op jit(solution)/shard_map/all_to_all | solution.py:68
  23.9 6.4 %all-to-all-done = bf16[4,4,2,16,128]{4,3,2,1,0:T(8,128)(2,1)S(1)} async-done(((bf16[4,4,2,16,128]{4,3,2,1,0:T(8,128)(2,1)}), bf16[4,4,2,16,128]{4,3,2,1,0:T(8,128)(2,1)S(1)}, u32[]{:S(2)}, u32[]{:S(2)}) %all-to-all-start) | async-done | bytes 131104 | tf_op jit(solution)/shard_map/all_to_all | solution.py:68
  30.3 3.3 %all-to-all-start.2 = ((bf16[4,4,2,16,128]{4,3,2,1,0:T(8,128)(2,1)}), bf16[4,4,2,16,128]{4,3,2,1,0:T(8,128)(2,1)S(1)}, u32[]{:S(2)}, u32[]{:S(2)}) async-start(bf16[4,4,2,16,128]{4,3,2,1,0:T(8,128)(2,1)} %copy.33), calls=%async_computation.2 | async-start | bytes 262144 | tf_op jit(solution)/shard_map/all_to_all | solution.py:72
  33.6 6.5 %all_gather.7 = bf16[2,1024,128]{1,2,0:T(8,128)(2,1)S(1)} all-gather(bf16[2,256,128]{1,2,0:T(8,128)(2,1)S(1)} %copy.43), channel_id=1, replica_groups=mesh['groups'=2,'frame'=4,'quarter'=2,'sub'=2] {'quarter','sub'}, dimensions={1}, use_global_device_ids=true | all-gather | bytes 655360 | tf_op jit(solution)/shard_map/all_gather | solution.py:102
  40.1 0.0 all-to-all-done.2
  40.2 0.2 fusion.18
  40.4 0.1 fusion.8
  40.5 0.3 fusion.3
  40.7 0.7 %copy.36 = bf16[1,4,8,16,128]{4,3,1,0,2:T(8,128)(2,1)} copy(bf16[1,4,8,16,128]{4,3,2,1,0:T(8,128)(2,1)S(1)} %bitcast.44) | data formatting | bytes 262144 | tf_op jit(solution)/shard_map/reshape | solution.py:92
  41.4 5.0 %all-to-all-start.3 = ((bf16[1,4,8,16,128]{4,3,1,0,2:T(8,128)(2,1)}), bf16[1,4,8,16,128]{4,3,1,0,2:T(8,128)(2,1)S(1)}, u32[]{:S(2)}, u32[]{:S(2)}) async-start(bf16[1,4,8,16,128]{4,3,1,0,2:T(8,128)(2,1)} %copy.36), calls=%async_computation.3 | async-start | bytes 262144 | tf_op jit(solution)/shard_map/all_to_all | solution.py:94
  46.4 0.6 %fusion.4 = bf16[2,256,128]{1,2,0:T(8,128)(2,1)S(1)} fusion(bf16[2,1024,128]{1,2,0:T(8,128)(2,1)S(1)} %all_gather.7, f32[2,256,1024]{2,1,0:T(8,128)S(1)} %get-tuple-element.14, f32[2,256]{1,0:T(2,128)S(1)} %get-tuple-element.13, f32[2,256]{1,0:T(2,128)S(1)} %get-tuple-element.10, f32[2,256]{1,0:T(2,128)S(1)} %get-tuple-element.9), kind=kOutput, calls=%fused_computation.9 | convolution fusion | flops 135987200 | bytes 2758656 | tf_op jit(solution)/shard_map/frn,fnd->frd/dot_general | solution.py:20
  47.0 5.8 %all-to-all-done.3 = bf16[1,4,8,16,128]{4,3,1,0,2:T(8,128)(2,1)S(1)} async-done(((bf16[1,4,8,16,128]{4,3,1,0,2:T(8,128)(2,1)}), bf16[1,4,8,16,128]{4,3,1,0,2:T(8,128)(2,1)S(1)}, u32[]{:S(2)}, u32[]{:S(2)}) %all-to-all-start.3) | async-done | bytes 131104 | tf_op jit(solution)/shard_map/all_to_all | solution.py:94
  52.9 0.1 copy.39
  53.0 0.8 %copy.40 = bf16[2,256,256]{2,1,0:T(8,128)(2,1)} copy(bf16[2,256,256]{1,2,0:T(8,128)(2,1)S(1)} %pad_maximum_fusion) | data formatting | bytes 524288 | tf_op jit(solution)/shard_map/concatenate | solution.py:106
  (7 shorter events, 0.1 us)
Async XLA Ops:
  1.0 15.7 %copy-start = (bf16[2,256,256]{2,1,0:T(8,128)(2,1)S(1)}, bf16[2,256,256]{2,1,0:T(8,128)(2,1)}, u32[]{:S(2)}) copy-start(bf16[2,256,256]{2,1,0:T(8,128)(2,1)} %param.5) | copy-start | bytes 786436
  1.7 17.1 %all-to-all-start.1 = ((bf16[4,4,2,16,128]{4,3,2,1,0:T(8,128)(2,1)}), bf16[4,4,2,16,128]{4,3,2,1,0:T(8,128)(2,1)S(1)}, u32[]{:S(2)}, u32[]{:S(2)}) async-start(bf16[4,4,2,16,128]{4,3,2,1,0:T(8,128)(2,1)} %copy.31), calls=%async_computation.1 | async-start | bytes 262144 | tf_op jit(solution)/shard_map/all_to_all | solution.py:71
  8.0 8.9 %slice-start = ((bf16[2,256,256]{2,1,0:T(8,128)(2,1)}), bf16[2,256,128]{2,1,0:T(8,128)(2,1)S(1)}, s32[]{:S(2)}) async-start(bf16[2,256,256]{2,1,0:T(8,128)(2,1)} %param.3), calls=%async_computation.4 | async-start | bytes 262144 | tf_op jit(solution)/shard_map/slice | solution.py:63
  18.7 11.5 %all-to-all-start = ((bf16[4,4,2,16,128]{4,3,2,1,0:T(8,128)(2,1)}), bf16[4,4,2,16,128]{4,3,2,1,0:T(8,128)(2,1)S(1)}, u32[]{:S(2)}, u32[]{:S(2)}) async-start(bf16[4,4,2,16,128]{4,3,2,1,0:T(8,128)(2,1)} %copy.29), calls=%async_computation | async-start | bytes 262144 | tf_op jit(solution)/shard_map/all_to_all | solution.py:68
  30.3 9.9 %all-to-all-start.2 = ((bf16[4,4,2,16,128]{4,3,2,1,0:T(8,128)(2,1)}), bf16[4,4,2,16,128]{4,3,2,1,0:T(8,128)(2,1)S(1)}, u32[]{:S(2)}, u32[]{:S(2)}) async-start(bf16[4,4,2,16,128]{4,3,2,1,0:T(8,128)(2,1)} %copy.33), calls=%async_computation.2 | async-start | bytes 262144 | tf_op jit(solution)/shard_map/all_to_all | solution.py:72
  41.4 11.5 %all-to-all-start.3 = ((bf16[1,4,8,16,128]{4,3,1,0,2:T(8,128)(2,1)}), bf16[1,4,8,16,128]{4,3,1,0,2:T(8,128)(2,1)S(1)}, u32[]{:S(2)}, u32[]{:S(2)}) async-start(bf16[1,4,8,16,128]{4,3,1,0,2:T(8,128)(2,1)} %copy.36), calls=%async_computation.3 | async-start | bytes 262144 | tf_op jit(solution)/shard_map/all_to_all | solution.py:94
where the time goes:
time: 54.4 us; the launch traced here: 53.8 us
  starting transfers between devices  19.8 us (36%)
  blocking collectives  13.8 us (25%)
  waiting for transfers between devices  12.2 us (22%)
  local copies, waits for them, and re-layouts  4.8 us (9%)
  matrix products  2.5 us (5%)
  other arithmetic  0.58 us (1%)
    all_gather x1, blocking collectives, body(): lax.all_gather(key_spatial, ('quarter', 'sub'), axis=1, tiled=True)  7.29 us
    all_gather x1, blocking collectives, body(): lax.all_gather(value_spatial, ('quarter', 'sub'), axis=1, tiled=True)  6.5 us
    all_to_all x1, waiting for transfers between devices, body(): lax.all_to_all(to_strips(queries), 'frame', split_axis=0, concat_axis=2,...  6.41 us
    all_to_all x1, starting transfers between devices, body(): lax.all_to_all(to_strips(keys), 'frame', split_axis=0, concat_axis=2, til...  6.35 us
    all_to_all x1, waiting for transfers between devices, body(): lax.all_to_all(strip_out, 'frame', split_axis=2, concat_axis=0, tiled=True)  5.8 us
    all_to_all x1, starting transfers between devices, body(): lax.all_to_all(to_strips(queries), 'frame', split_axis=0, concat_axis=2,...  5.1 us
    all_to_all x1, starting transfers between devices, body(): lax.all_to_all(strip_out, 'frame', split_axis=2, concat_axis=0, tiled=True)  5.04 us
    all_to_all x1, starting transfers between devices, body(): lax.all_to_all(to_strips(values), 'frame', split_axis=0, concat_axis=2, t...  3.33 us
  transfers between devices with their start and end apart: 4, of which 2 were waited for; matrix products, arithmetic and copies ran while one was open for 7% of the time, Pallas kernels for 0%

commit v1 on v0

--- a/solution.py
+++ b/solution.py
@@ -5,6 +5,33 @@
 from jax.sharding import PartitionSpec as P
 
 STRIP = 16
+
+
+def answer_arrays(patch, link_axis, dim_at):
+    later = lax.axis_size(link_axis)
+    found_now = lax.axis_index(link_axis)
+    local_out, placed, block_next = (later, found_now, patch.shape[dim_at])
+    made = [q * local_out if i == dim_at else q for i, q in enumerate(patch.shape)]
+    outer = jnp.zeros(made, patch.dtype)
+    f_now = u_next = patch
+    v_now = lax.dynamic_update_slice_in_dim(outer, patch, placed * block_next, axis=dim_at)
+    for d in range(1, local_out // 2 + 1):
+        piece_next = range(local_out)
+        k_now = map(lambda i: (i, (i + 1) % local_out), piece_next)
+        y1 = list(k_now)
+        f_now = lax.ppermute(f_now, link_axis, perm=y1)
+        v_now = lax.dynamic_update_slice_in_dim(
+            v_now, f_now, (placed - d) % local_out * block_next, axis=dim_at
+        )
+        if 2 * d < local_out:
+            out_arr = range(local_out)
+            mixed_arr = map(lambda i: (i, (i - 1) % local_out), out_arr)
+            new = list(mixed_arr)
+            u_next = lax.ppermute(u_next, link_axis, new)
+            v_now = lax.dynamic_update_slice_in_dim(
+                v_now, u_next, (placed + d) % local_out * block_next, axis=dim_at
+            )
+    return v_now
 
 
 def partial_attend(query_rows, key_rows, value_rows, running, score_scale):
@@ -98,7 +125,7 @@
         score_scale,
         empty_state(query_spatial),
         (
-            lax.all_gather(key_spatial, ("quarter", "sub"), axis=1, tiled=True),
+            answer_arrays(key_spatial, ("quarter", "sub"), 1),
             lax.all_gather(value_spatial, ("quarter", "sub"), axis=1, tiled=True),
         ),
     )

time: 54.4 us -> 49.2 us (0.904)
  blocking collectives: 13.8 us -> 7.17 us
  local copies, waits for them, and re-layouts: 4.8 us -> 5.96 us
  waiting for transfers between devices: 12.2 us -> 13.3 us
  matrix products: 2.5 us -> 1.43 us
    all_gather x1 -> x0, blocking collectives: 7.29 us -> none  [body(): lax.all_gather(key_spatial, ('quarter', 'sub'), axis=1, tiled=True)]
    all_to_all x1, waiting for transfers between devices: 6.41 us -> 0.01 us  [body(): lax.all_to_all(to_strips(queries), 'frame', split_axis=0, concat_axis=2,...]
    all_to_all x1, waiting for transfers between devices: 0.01 us -> 6.37 us  [body(): lax.all_to_all(to_strips(keys), 'frame', split_axis=0, concat_axis=2, til...]
    all_to_all x1, starting transfers between devices: 3.33 us -> 6.35 us  [body(): lax.all_to_all(to_strips(values), 'frame', split_axis=0, concat_axis=2, t...]
    all_to_all x1, waiting for transfers between devices: 0.01 us -> 2.38 us  [body(): lax.all_to_all(to_strips(values), 'frame', split_axis=0, concat_axis=2, t...]
    ppermute x0 -> x3, starting transfers between devices: none -> 2.14 us  [the longest x1 1.73 us: answer_arrays(): u_next = lax.ppermute(u_next, link_axis, new)]
    all_to_all x1, starting transfers between devices: 5.1 us -> 3.32 us  [body(): lax.all_to_all(to_strips(queries), 'frame', split_axis=0, concat_axis=2,...]
    all_to_all x1, starting transfers between devices: 5.04 us -> 3.33 us  [body(): lax.all_to_all(strip_out, 'frame', split_axis=2, concat_axis=0, tiled=True)]
  transfers between devices with their start and end apart: 4 -> 7, of which waited for: 2 -> 3; matrix products, arithmetic and copies ran while one was open for 7% -> 11% of each run, Pallas kernels for 0% -> 0%
where the time goes in v1:
time: 49.2 us; the launch traced here: 48.6 us
  starting transfers between devices  20.2 us (41%)
  waiting for transfers between devices  13.3 us (27%)
  blocking collectives  7.17 us (15%)
  local copies, waits for them, and re-layouts  5.96 us (12%)
  matrix products  1.43 us (3%)
    all_gather x1, blocking collectives, body(): lax.all_gather(value_spatial, ('quarter', 'sub'), axis=1, tiled=True)  7.17 us
    all_to_all x1, waiting for transfers between devices, body(): lax.all_to_all(to_strips(keys), 'frame', split_axis=0, concat_axis=2, til...  6.37 us
    all_to_all x1, starting transfers between devices, body(): lax.all_to_all(to_strips(values), 'frame', split_axis=0, concat_axis=2, t...  6.35 us
    all_to_all x1, starting transfers between devices, body(): lax.all_to_all(to_strips(keys), 'frame', split_axis=0, concat_axis=2, til...  5.04 us
    all_to_all x1, waiting for transfers between devices, body(): lax.all_to_all(strip_out, 'frame', split_axis=2, concat_axis=0, tiled=True)  4.49 us
    all_to_all x1, starting transfers between devices, body(): lax.all_to_all(strip_out, 'frame', split_axis=2, concat_axis=0, tiled=True)  3.33 us
    all_to_all x1, starting transfers between devices, body(): lax.all_to_all(to_strips(queries), 'frame', split_axis=0, concat_axis=2,...  3.32 us
    all_to_all x1, waiting for transfers between devices, body(): lax.all_to_all(to_strips(values), 'frame', split_axis=0, concat_axis=2, t...  2.38 us
  transfers between devices with their start and end apart: 7, of which 3 were waited for; matrix products, arithmetic and copies ran while one was open for 11% of the time, Pallas kernels for 0%

profile of v1, /device:TPU:0, one launch (start us, length us, event | category | flops | bytes accessed | tf_op | source)
XLA Modules:
  0.0 48.6 jit_solution(7288028177025399771)
XLA Ops:
  0.0 0.0 slice-start
  0.0 1.0 %fusion.17 = (bf16[2,256,128]{2,1,0:T(8,128)(2,1)S(1)}, bf16[2,256,128]{2,1,0:T(8,128)(2,1)S(1)}) fusion(bf16[2,256,256]{2,1,0:T(8,128)(2,1)} %param.5), kind=kLoop, calls=%fused_computation.26 | loop fusion | bytes 524288 | tf_op jit(solution)/shard_map/slice | solution.py:85
  1.0 0.7 %copy.37 = bf16[4,4,2,16,128]{4,3,2,1,0:T(8,128)(2,1)} copy(bf16[4,4,2,16,128]{4,3,1,0,2:T(8,128)(2,1)S(1)} %bitcast.54) | data formatting | bytes 262144 | tf_op jit(solution)/shard_map/transpose | solution.py:93
  1.7 6.3 %all-to-all-start.2 = ((bf16[4,4,2,16,128]{4,3,2,1,0:T(8,128)(2,1)}), bf16[4,4,2,16,128]{4,3,2,1,0:T(8,128)(2,1)S(1)}, u32[]{:S(2)}, u32[]{:S(2)}) async-start(bf16[4,4,2,16,128]{4,3,2,1,0:T(8,128)(2,1)} %copy.37), calls=%async_computation.2 | async-start | bytes 262144 | tf_op jit(solution)/shard_map/all_to_all | solution.py:99
  8.0 0.1 broadcast_in_dim.7
  8.1 1.0 %fusion.18 = (bf16[2,256,128]{2,1,0:T(8,128)(2,1)S(1)}, bf16[2,1024,128]{2,1,0:T(8,128)(2,1)S(1)}, bf16[2,256,128]{2,1,0:T(8,128)(2,1)S(1)}) fusion(bf16[2,256,256]{2,1,0:T(8,128)(2,1)} %param.4, bf16[2,1024,128]{2,1,0:T(8,128)(2,1)S(1)} %broadcast_in_dim.7, s32[]{:T(128)S(6)} %select_n.27), kind=kLoop, calls=%fused_computation.27 | loop fusion | bytes 655364 | tf_op jit(solution)/shard_map/slice | solution.py:84
  9.1 0.1 collective-permute-start
  9.2 1.7 %collective-permute-start.1 = (bf16[2,256,128]{2,1,0:T(8,128)(2,1)S(1)}, bf16[2,256,128]{2,1,0:T(8,128)(2,1)S(1)}, u32[]{:S(2)}, u32[]{:S(2)}) collective-permute-start(bf16[2,256,128]{2,1,0:T(8,128)(2,1)S(1)} %get-tuple-element.7), channel_id=1, source_target_pairs={{0,3},{1,0},{2,1},{3,2},{4,7},{5,4},{6,5},{7,6},{8,11},{9,8},{10,9... | collective-permute-start | bytes 393224 | tf_op jit(solution)/shard_map/ppermute | solution.py:30
  10.9 0.0 slice-done
  10.9 0.7 %copy.33 = bf16[4,4,2,16,128]{4,3,2,1,0:T(8,128)(2,1)} copy(bf16[4,4,2,16,128]{4,3,1,0,2:T(8,128)(2,1)S(1)} %bitcast.50) | data formatting | bytes 262144 | tf_op jit(solution)/shard_map/transpose | solution.py:93
  11.6 0.1 copy.48
  11.7 2.4 %all-to-all-done.2 = bf16[4,4,2,16,128]{4,3,2,1,0:T(8,128)(2,1)S(1)} async-done(((bf16[4,4,2,16,128]{4,3,2,1,0:T(8,128)(2,1)}), bf16[4,4,2,16,128]{4,3,2,1,0:T(8,128)(2,1)S(1)}, u32[]{:S(2)}, u32[]{:S(2)}) %all-to-all-start.2) | async-done | bytes 131104 | tf_op jit(solution)/shard_map/all_to_all | solution.py:99
  14.1 3.3 %all-to-all-start = ((bf16[4,4,2,16,128]{4,3,2,1,0:T(8,128)(2,1)}), bf16[4,4,2,16,128]{4,3,2,1,0:T(8,128)(2,1)S(1)}, u32[]{:S(2)}, u32[]{:S(2)}) async-start(bf16[4,4,2,16,128]{4,3,2,1,0:T(8,128)(2,1)} %copy.33), calls=%async_computation | async-start | bytes 262144 | tf_op jit(solution)/shard_map/all_to_all | solution.py:95
  17.4 7.2 %all_gather.3 = bf16[2,1024,128]{1,2,0:T(8,128)(2,1)S(1)} all-gather(bf16[2,256,128]{1,2,0:T(8,128)(2,1)S(1)} %copy.48), channel_id=1, replica_groups=mesh['groups'=2,'frame'=4,'quarter'=2,'sub'=2] {'quarter','sub'}, dimensions={1}, use_global_device_ids=true | all-gather | bytes 655360 | tf_op jit(solution)/shard_map/all_gather | solution.py:129
  24.6 0.7 %copy.35 = bf16[4,4,2,16,128]{4,3,2,1,0:T(8,128)(2,1)} copy(bf16[4,4,2,16,128]{4,3,1,0,2:T(8,128)(2,1)S(1)} %bitcast.51) | data formatting | bytes 262144 | tf_op jit(solution)/shard_map/transpose | solution.py:93
  25.3 0.0 copy-start
  25.3 0.0 collective-permute-done
  25.3 0.3 collective-permute-start.2
  25.6 0.0 all-to-all-done
  25.6 5.0 %all-to-all-start.1 = ((bf16[4,4,2,16,128]{4,3,2,1,0:T(8,128)(2,1)}), bf16[4,4,2,16,128]{4,3,2,1,0:T(8,128)(2,1)S(1)}, u32[]{:S(2)}, u32[]{:S(2)}) async-start(bf16[4,4,2,16,128]{4,3,2,1,0:T(8,128)(2,1)} %copy.35), calls=%async_computation.1 | async-start | bytes 262144 | tf_op jit(solution)/shard_map/all_to_all | solution.py:98
  30.7 0.0 collective-permute-done.1
  30.8 6.4 %all-to-all-done.1 = bf16[4,4,2,16,128]{4,3,2,1,0:T(8,128)(2,1)S(1)} async-done(((bf16[4,4,2,16,128]{4,3,2,1,0:T(8,128)(2,1)}), bf16[4,4,2,16,128]{4,3,2,1,0:T(8,128)(2,1)S(1)}, u32[]{:S(2)}, u32[]{:S(2)}) %all-to-all-start.1) | async-done | bytes 131104 | tf_op jit(solution)/shard_map/all_to_all | solution.py:98
  37.2 0.2 fusion.19
  37.4 0.1 fusion.7
  37.5 0.3 fusion.3
  37.7 0.7 %copy.40 = bf16[1,4,8,16,128]{4,3,1,0,2:T(8,128)(2,1)} copy(bf16[1,4,8,16,128]{4,3,2,1,0:T(8,128)(2,1)S(1)} %bitcast.56) | data formatting | bytes 262144 | tf_op jit(solution)/shard_map/reshape | solution.py:119
  38.4 3.3 %all-to-all-start.3 = ((bf16[1,4,8,16,128]{4,3,1,0,2:T(8,128)(2,1)}), bf16[1,4,8,16,128]{4,3,1,0,2:T(8,128)(2,1)S(1)}, u32[]{:S(2)}, u32[]{:S(2)}) async-start(bf16[1,4,8,16,128]{4,3,1,0,2:T(8,128)(2,1)} %copy.40), calls=%async_computation.3 | async-start | bytes 262144 | tf_op jit(solution)/shard_map/all_to_all | solution.py:121
  41.7 0.0 collective-permute-done.2
  41.8 0.0 copy-done
  41.8 0.4 bitcast_reduce_fusion
  42.2 0.4 fusion.1
  42.6 0.5 %divide_convert_fusion = bf16[2,256,128]{1,2,0:T(8,128)(2,1)S(1)} fusion(f32[2,256]{1,0:T(2,128)S(1)} %get-tuple-element.11, bf16[2,1024,128]{1,2,0:T(8,128)(2,1)S(1)} %all_gather.3, f32[2,1024,256]{2,1,0:T(8,128)S(1)} %get-tuple-element.15, f32[2,256]{1,0:T(2,128)S(1)} %get-tuple-element.14, f32[2,256]{1,0:T(2,128)S(1)} %get-tuple-element.10), kind=kOutput, calls=%fused_computation.13 | convolution fusion | flops 135987200 | bytes 2758656 | tf_op jit(solution)/shard_map/frn,fnd->frd/dot_general | solution.py:47
  43.1 4.5 %all-to-all-done.3 = bf16[1,4,8,16,128]{4,3,1,0,2:T(8,128)(2,1)S(1)} async-done(((bf16[1,4,8,16,128]{4,3,1,0,2:T(8,128)(2,1)}), bf16[1,4,8,16,128]{4,3,1,0,2:T(8,128)(2,1)S(1)}, u32[]{:S(2)}, u32[]{:S(2)}) %all-to-all-start.3) | async-done | bytes 131104 | tf_op jit(solution)/shard_map/all_to_all | solution.py:121
  47.6 0.1 copy.43
  47.8 0.8 %copy.44 = bf16[2,256,256]{2,1,0:T(8,128)(2,1)} copy(bf16[2,256,256]{1,2,0:T(8,128)(2,1)S(1)} %pad_maximum_fusion) | data formatting | bytes 524288 | tf_op jit(solution)/shard_map/concatenate | solution.py:133
  (9 shorter events, 0.1 us)
Async XLA Ops:
  0.0 10.9 %slice-start = ((bf16[2,256,256]{2,1,0:T(8,128)(2,1)}), bf16[2,256,128]{2,1,0:T(8,128)(2,1)S(1)}, s32[]{:S(2)}) async-start(bf16[2,256,256]{2,1,0:T(8,128)(2,1)} %param.3), calls=%async_computation.4 | async-start | bytes 262144 | tf_op jit(solution)/shard_map/slice | solution.py:90
  1.7 12.4 %all-to-all-start.2 = ((bf16[4,4,2,16,128]{4,3,2,1,0:T(8,128)(2,1)}), bf16[4,4,2,16,128]{4,3,2,1,0:T(8,128)(2,1)S(1)}, u32[]{:S(2)}, u32[]{:S(2)}) async-start(bf16[4,4,2,16,128]{4,3,2,1,0:T(8,128)(2,1)} %copy.37), calls=%async_computation.2 | async-start | bytes 262144 | tf_op jit(solution)/shard_map/all_to_all | solution.py:99
  9.1 16.1 %collective-permute-start = (bf16[2,256,128]{2,1,0:T(8,128)(2,1)S(1)}, bf16[2,256,128]{2,1,0:T(8,128)(2,1)S(1)}, u32[]{:S(2)}, u32[]{:S(2)}) collective-permute-start(bf16[2,256,128]{2,1,0:T(8,128)(2,1)S(1)} %get-tuple-element.7), channel_id=1, source_target_pairs={{0,1},{1,2},{2,3},{3,0},{4,5},{5,6},{6,7},{7,4},{8,9},{9,10},{10,1... | collective-permute-start | bytes 393224 | tf_op jit(solution)/shard_map/ppermute | solution.py:22
  9.2 21.5 %collective-permute-start.1 = (bf16[2,256,128]{2,1,0:T(8,128)(2,1)S(1)}, bf16[2,256,128]{2,1,0:T(8,128)(2,1)S(1)}, u32[]{:S(2)}, u32[]{:S(2)}) collective-permute-start(bf16[2,256,128]{2,1,0:T(8,128)(2,1)S(1)} %get-tuple-element.7), channel_id=1, source_target_pairs={{0,3},{1,0},{2,1},{3,2},{4,7},{5,4},{6,5},{7,6},{8,11},{9,8},{10,9... | collective-permute-start | bytes 393224 | tf_op jit(solution)/shard_map/ppermute | solution.py:30
  14.1 11.5 %all-to-all-start = ((bf16[4,4,2,16,128]{4,3,2,1,0:T(8,128)(2,1)}), bf16[4,4,2,16,128]{4,3,2,1,0:T(8,128)(2,1)S(1)}, u32[]{:S(2)}, u32[]{:S(2)}) async-start(bf16[4,4,2,16,128]{4,3,2,1,0:T(8,128)(2,1)} %copy.33), calls=%async_computation | async-start | bytes 262144 | tf_op jit(solution)/shard_map/all_to_all | solution.py:95
  25.3 16.5 %copy-start = (bf16[2,256,256]{2,1,0:T(8,128)(2,1)S(1)}, bf16[2,256,256]{2,1,0:T(8,128)(2,1)}, u32[]{:S(2)}) copy-start(bf16[2,256,256]{2,1,0:T(8,128)(2,1)} %param.3) | copy-start | bytes 786436
  25.3 16.4 %collective-permute-start.2 = (bf16[2,256,128]{2,1,0:T(8,128)(2,1)S(1)}, bf16[2,256,128]{2,1,0:T(8,128)(2,1)S(1)}, u32[]{:S(2)}, u32[]{:S(2)}) collective-permute-start(bf16[2,256,128]{2,1,0:T(8,128)(2,1)S(1)} %collective-permute-done), channel_id=1, source_target_pairs={{0,1},{1,2},{2,3},{3,0},{4,5},{5,6},{6,7},{7,4},{8,9},{9,10},{10,1... | collective-permute-start | bytes 393224 | tf_op jit(solution)/shard_map/ppermute | solution.py:22
  25.6 11.5 %all-to-all-start.1 = ((bf16[4,4,2,16,128]{4,3,2,1,0:T(8,128)(2,1)}), bf16[4,4,2,16,128]{4,3,2,1,0:T(8,128)(2,1)S(1)}, u32[]{:S(2)}, u32[]{:S(2)}) async-start(bf16[4,4,2,16,128]{4,3,2,1,0:T(8,128)(2,1)} %copy.35), calls=%async_computation.1 | async-start | bytes 262144 | tf_op jit(solution)/shard_map/all_to_all | solution.py:98
  38.4 9.2 %all-to-all-start.3 = ((bf16[1,4,8,16,128]{4,3,1,0,2:T(8,128)(2,1)}), bf16[1,4,8,16,128]{4,3,1,0,2:T(8,128)(2,1)S(1)}, u32[]{:S(2)}, u32[]{:S(2)}) async-start(bf16[1,4,8,16,128]{4,3,1,0,2:T(8,128)(2,1)} %copy.40), calls=%async_computation.3 | async-start | bytes 262144 | tf_op jit(solution)/shard_map/all_to_all | solution.py:121
